TPU v7x, 128 devices: a whole 4x4x4 slice. The times are simulated.
128 devices in a mesh: snap: 4 (over z_lo, core), pts: 32 (over z_hi, x, y).
Axes of the slice: x: 4, y: 4, z: 4 (z_hi: 2, z_lo: 2; z = z_hi * 2 + z_lo), core: 2. Of those that a mesh axis runs over, the one named last changes fastest.
Arguments:
- strains: bfloat16 [6, 512, 131072], P(None, 'snap', 'pts'), may hold values from -3 to 3
- moduli: float32 [2, 131072], P(None, 'pts'), may hold values from 0.5 to 2
- range_test: bfloat16 [131072, 256], P('pts'), may hold values from -0.015625 to 0.015625
- corange_test: bfloat16 [256, 512], replicated, may hold values from -0.25 to 0.25
- core_left: float32 [512, 512], P(None, 'snap'), may hold values from -0.25 to 0.25
- core_right: bfloat16 [512, 131072], P(None, 'pts'), may hold values from -0.015625 to 0.015625
Outputs:
- range_sketch: float32 [512, 256], P('snap')
- corange_sketch: float32 [256, 131072], P('snap', 'pts')
- core_sketch: float32 [512, 512], replicated
All inputs are finite; a program needn't handle non-finite values.
Results may differ from a plain program's by a relative error of at most 0.0031.
Values may be sent and summed in bfloat16 or wider, within the bound.
A program may use at most 64 MiB of HBM per device.

v0:
```python
import math
import jax
import jax.numpy as jnp
from jax import lax
from jax.sharding import PartitionSpec as P


def energy_field(strains, moduli):
    strain_xx = strains[0].astype(jnp.float32)
    strain_yy = strains[1].astype(jnp.float32)
    strain_zz = strains[2].astype(jnp.float32)
    strain_xy = strains[3].astype(jnp.float32)
    strain_yz = strains[4].astype(jnp.float32)
    strain_xz = strains[5].astype(jnp.float32)
    lame_first = moduli[0][None, :]
    shear_mod = moduli[1][None, :]
    strain_trace = strain_xx + strain_yy + strain_zz
    mean_strain = strain_trace / 3.0
    dev_xx = strain_xx - mean_strain
    dev_yy = strain_yy - mean_strain
    dev_zz = strain_zz - mean_strain
    dev_square = (
        dev_xx * dev_xx
        + dev_yy * dev_yy
        + dev_zz * dev_zz
        + 2.0 * (strain_xy * strain_xy + strain_yz * strain_yz + strain_xz * strain_xz)
    ) / 6.0
    dev_norm = jnp.sqrt(dev_square)
    dev_det = (
        dev_xx * (dev_yy * dev_zz - strain_yz * strain_yz)
        - strain_xy * (strain_xy * dev_zz - strain_yz * strain_xz)
        + strain_xz * (strain_xy * strain_yz - dev_yy * strain_xz)
    )
    sine_part = jnp.sqrt(
        jnp.maximum(4.0 * dev_square * dev_square * dev_square - dev_det * dev_det, 0.0)
    )
    angle_third = jnp.arctan2(sine_part, dev_det) / 3.0
    positive_trace = jnp.maximum(strain_trace, 0.0)
    density = 0.5 * lame_first * positive_trace * positive_trace
    for order in range(3):
        principal = mean_strain + 2.0 * dev_norm * jnp.cos(
            angle_third - 2.0 * math.pi * order / 3.0
        )
        positive = jnp.maximum(principal, 0.0)
        density = density + shear_mod * positive * positive
    return density.astype(jnp.bfloat16)


def per_device(strains, moduli, range_test, corange_test, core_left, core_right):
    energy = energy_field(strains, moduli)
    snap_rows = energy.shape[0]
    range_part = jnp.dot(energy, range_test, preferred_element_type=jnp.float32)
    cross_part = lax.dot_general(
        energy, core_right, (((1,), (1,)), ((), ())), preferred_element_type=jnp.float32
    )
    range_sketch = lax.psum(range_part, "pts")
    core_share = jnp.dot(core_left, cross_part, precision=lax.Precision.HIGHEST)
    core_sketch = lax.psum(core_share, ("snap", "pts"))
    own_cols = lax.dynamic_slice_in_dim(
        corange_test, lax.axis_index("snap") * snap_rows, snap_rows, 1
    )
    corange_sketch = lax.psum_scatter(
        jnp.dot(own_cols, energy, preferred_element_type=jnp.float32),
        "snap",
        scatter_dimension=0,
        tiled=True,
    )
    return (range_sketch, corange_sketch, core_sketch)


def solution(mesh):
    in_specs = (
        P(None, "snap", "pts"),
        P(None, "pts"),
        P("pts", None),
        P(),
        P(None, "snap"),
        P(None, "pts"),
    )
    out_specs = (P("snap", None), P("snap", "pts"), P())
    return jax.shard_map(
        per_device, mesh=mesh, in_specs=in_specs, out_specs=out_specs, check_vma=False
    )
```

profile of v0, /device:TPU:0, one launch (start us, length us, event | category | flops | bytes accessed | tf_op | source)
XLA Modules:
  0.0 557.0 jit_solution(8219614878723953401)
XLA Ops:
  8.0 0.0 copy-start
  8.0 0.0 all-reduce.5.cloned.1.call-start
  8.1 0.9 slice_multiply_fusion
  9.0 0.0 copy-start.1
  9.0 31.8 %fusion.11 = bf16[128,4096]{1,0:T(8,128)(2,1)S(1)} fusion(bf16[6,128,4096]{2,1,0:T(8,128)(2,1)} %param.6, f32[4096]{0:T(1024)S(1)} %bitcast.30, f32[4096]{0:T(1024)S(1)} %bitcast.29), kind=kLoop, calls=%fused_computation.30 | loop fusion | flops 36700160 | bytes 7372800 | tf_op jit(solution)/shard_map/convert_element_type | solution.py:46
  40.9 0.0 copy-done.1
  40.9 0.0 copy-start.2
  40.9 1.5 fusion.27
  42.4 0.0 copy-done.2
  42.4 2.0 convolution_bitcast_fusion
  44.4 0.0 all-reduce.5.cloned.1.call-update
  44.5 0.0 all-reduce.3.cloned.1.call-start
  44.5 0.0 copy-done
  44.5 1.1 fusion.26
  45.6 0.0 all-reduce.3.cloned.1.call-update
  45.7 0.0 reduce-scatter.2.cloned.1.call-start
  45.7 3.5 fusion.23
  49.2 0.0 reduce-scatter.2.cloned.1.call-update
  49.2 170.6 %all-reduce.5.cloned.1.call-done = f32[512,512]{0,1:T(8,128)} async-done(((f32[512,512]{0,1:T(8,128)}), f32[512,512]{0,1:T(8,128)}) %all-reduce.5.cloned.1.call-update) | async-done | bytes 1048592 | tf_op jit(solution)/shard_map/psum | solution.py:58
  219.8 2.5 copy.9
  222.3 325.7 %all-reduce.3.cloned.1.call-done = f32[128,256]{1,0:T(8,128)} async-done(((f32[128,256]{1,0:T(8,128)}), f32[128,256]{1,0:T(8,128)}) %all-reduce.3.cloned.1.call-update) | async-done | bytes 131088 | tf_op jit(solution)/shard_map/psum | solution.py:56
  548.0 0.0 reduce-scatter.2.cloned.1.call-done
  548.0 1.6 copy.12
Async XLA Ops:
  8.0 36.5 %copy-start = (bf16[4096,256]{1,0:T(8,128)(2,1)S(1)}, bf16[4096,256]{1,0:T(8,128)(2,1)}, u32[]{:S(2)}) copy-start(bf16[4096,256]{1,0:T(8,128)(2,1)} %param.8) | copy-start | bytes 6291460
  8.0 211.8 %all-reduce.5.cloned.1.call-start = ((), (), s32[]{:S(2)}) async-start(), calls=%async_computation.3 | async-start | bytes 2097152 | tf_op jit(solution)/shard_map/psum | solution.py:58
  9.0 31.9 %copy-start.1 = (bf16[512,4096]{1,0:T(8,128)(2,1)S(1)}, bf16[512,4096]{1,0:T(8,128)(2,1)}, u32[]{:S(2)}) copy-start(bf16[512,4096]{1,0:T(8,128)(2,1)} %param.11) | copy-start | bytes 12582916
  40.9 1.6 copy-start.2
  44.5 503.6 %all-reduce.3.cloned.1.call-start = ((), (), s32[]{:S(2)}) async-start(), calls=%async_computation.1 | async-start | bytes 262144 | tf_op jit(solution)/shard_map/psum | solution.py:56
  45.7 502.4 %reduce-scatter.2.cloned.1.call-start = ((), (), s32[]{:S(2)}) async-start(), calls=%async_computation.2 | async-start | bytes 5242880 | tf_op jit(solution)/shard_map/reduce_scatter | solution.py:62
Sparse Core Ops, SparseCore 0:
  44.6 175.1 all-reduce.4
  222.8 325.1 all-reduce.2
Sparse Core Ops, SparseCore 1:
  49.3 47.8 reduce-scatter.1
where the time goes:
time: 557 us
  waiting for transfers between devices  496 us (89%)
  other arithmetic  32.8 us (6%)
  between operations  15.6 us (3%)
  matrix products  8.11 us (1%)
    psum x1, waiting for transfers between devices, per_device(): range_sketch = lax.psum(range_part, 'pts')  326 us
    psum x1, waiting for transfers between devices, per_device(): core_sketch = lax.psum(core_share, ('snap', 'pts'))  171 us
    convert_element_type x1, other arithmetic, energy_field(): return density.astype(jnp.bfloat16)  31.8 us
  transfers between devices with their start and end apart: 3, of which 2 were waited for; matrix products, arithmetic and copies ran while one was open for 1% of the time, Pallas kernels for 0%

commit v1 on v0

--- a/solution.py
+++ b/solution.py
@@ -55,7 +55,8 @@
     )
     range_sketch = lax.psum(range_part, "pts")
     core_share = jnp.dot(core_left, cross_part, precision=lax.Precision.HIGHEST)
-    core_sketch = lax.psum(core_share, ("snap", "pts"))
+    half = lax.psum(core_share, "pts")
+    core_sketch = lax.psum(half, "snap")
     own_cols = lax.dynamic_slice_in_dim(
         corange_test, lax.axis_index("snap") * snap_rows, snap_rows, 1
     )

time: 557 us -> 498 us (0.89)
  waiting for transfers between devices: 496 us -> 438 us
    psum x1, waiting for transfers between devices: 171 us -> 38.9 us  [per_device(): core_sketch = lax.psum(half, 'snap')]
    reduce_scatter x1, waiting for transfers between devices: 0.01 us -> 46.9 us  [per_device(): lax.psum_scatter(jnp.dot(own_cols, energy, preferred_element_type=jnp.flo...]
    psum x1, waiting for transfers between devices: 326 us -> 352 us  [per_device(): range_sketch = lax.psum(range_part, 'pts')]
  transfers between devices with their start and end apart: 3 -> 3, of which waited for: 2 -> 3; matrix products, arithmetic and copies ran while one was open for 1% -> 1% of each run, Pallas kernels for 0% -> 0%
where the time goes in v1:
time: 498 us; the launch traced here: 496 us
  waiting for transfers between devices  438 us (88%)
  other arithmetic  32.8 us (7%)
  between operations  13.8 us (3%)
  matrix products  8.11 us (2%)
    psum x1, waiting for transfers between devices, per_device(): range_sketch = lax.psum(range_part, 'pts')  352 us
    reduce_scatter x1, waiting for transfers between devices, per_device(): lax.psum_scatter(jnp.dot(own_cols, energy, preferred_element_type=jnp.flo...  46.9 us
    psum x1, waiting for transfers between devices, per_device(): core_sketch = lax.psum(half, 'snap')  38.9 us
    convert_element_type x1, other arithmetic, energy_field(): return density.astype(jnp.bfloat16)  31.8 us
  transfers between devices with their start and end apart: 3, of which 3 were waited for; matrix products, arithmetic and copies ran while one was open for 1% of the time, Pallas kernels for 0%

profile of v1, /device:TPU:0, one launch (start us, length us, event | category | flops | bytes accessed | tf_op | source)
XLA Modules:
  0.0 496.4 jit_solution(10489692461443247661)
XLA Ops:
  7.2 0.0 copy-start
  7.2 0.0 all-reduce.6.cloned.1.call-start
  7.2 0.9 slice_multiply_fusion
  8.2 0.0 copy-start.1
  8.2 31.8 %fusion.11 = bf16[128,4096]{1,0:T(8,128)(2,1)S(1)} fusion(bf16[6,128,4096]{2,1,0:T(8,128)(2,1)} %param.6, f32[4096]{0:T(1024)S(1)} %bitcast.30, f32[4096]{0:T(1024)S(1)} %bitcast.29), kind=kLoop, calls=%fused_computation.30 | loop fusion | flops 36700160 | bytes 7372800 | tf_op jit(solution)/shard_map/convert_element_type | solution.py:46
  40.0 0.0 copy-done.1
  40.1 1.5 fusion.27
  41.6 0.0 copy-done
  41.6 0.0 copy-start.2
  41.6 1.1 fusion.26
  42.7 0.0 copy-done.2
  42.7 2.0 convolution_bitcast_fusion
  44.7 0.0 all-reduce.6.cloned.1.call-update
  44.7 0.0 all-reduce.4.cloned.1.call-start
  44.8 352.5 %all-reduce.6.cloned.1.call-done = (f32[128,256]{1,0:T(8,128)}, f32[512,512]{0,1:T(8,128)}) async-done(((f32[128,256]{1,0:T(8,128)}, f32[512,512]{0,1:T(8,128)}), (f32[128,256]{1,0:T(8,128)}, f32[512,512]{0,1:T(8,128)})) %all-reduce.6.cloned.1.call-update) | async-done | bytes 1179664 | tf_op jit(solution)/shard_map/psum | solution.py:56
  397.3 0.0 all-reduce.4.cloned.1.call-update
  397.3 0.0 reduce-scatter.2.cloned.1.call-start
  397.3 3.5 fusion.23
  400.8 0.0 reduce-scatter.2.cloned.1.call-update
  400.8 0.0 copy-start.3
  400.8 38.9 %all-reduce.4.cloned.1.call-done = f32[512,512]{0,1:T(8,128)} async-done(((f32[512,512]{0,1:T(8,128)}), f32[512,512]{0,1:T(8,128)}) %all-reduce.4.cloned.1.call-update) | async-done | bytes 1048592 | tf_op jit(solution)/shard_map/psum | solution.py:59
  439.7 2.5 copy.9
  442.3 46.9 %reduce-scatter.2.cloned.1.call-done = f32[64,4096]{1,0:T(8,128)} async-done(((f32[256,4096]{1,0:T(8,128)}), f32[64,4096]{1,0:T(8,128)}) %reduce-scatter.2.cloned.1.call-update) | async-done | bytes 1048592 | tf_op jit(solution)/shard_map/reduce_scatter | solution.py:63
  489.2 0.0 copy-done.3
  489.2 0.7 copy.13
Async XLA Ops:
  7.2 34.4 %copy-start = (bf16[4096,256]{1,0:T(8,128)(2,1)S(1)}, bf16[4096,256]{1,0:T(8,128)(2,1)}, u32[]{:S(2)}) copy-start(bf16[4096,256]{1,0:T(8,128)(2,1)} %param.8) | copy-start | bytes 6291460
  7.2 390.1 %all-reduce.6.cloned.1.call-start = ((), (), s32[]{:S(2)}) async-start(), calls=%async_computation.3 | async-start | bytes 2359296 | tf_op jit(solution)/shard_map/psum | solution.py:56
  8.2 31.9 %copy-start.1 = (bf16[512,4096]{1,0:T(8,128)(2,1)S(1)}, bf16[512,4096]{1,0:T(8,128)(2,1)}, u32[]{:S(2)}) copy-start(bf16[512,4096]{1,0:T(8,128)(2,1)} %param.11) | copy-start | bytes 12582916
  41.6 1.1 copy-start.2
  44.7 395.0 %all-reduce.4.cloned.1.call-start = ((), (), s32[]{:S(2)}) async-start(), calls=%async_computation.2 | async-start | bytes 2097152 | tf_op jit(solution)/shard_map/psum | solution.py:59
  397.3 91.9 %reduce-scatter.2.cloned.1.call-start = ((), (), s32[]{:S(2)}) async-start(), calls=%async_computation.1 | async-start | bytes 5242880 | tf_op jit(solution)/shard_map/reduce_scatter | solution.py:63
  400.8 88.4 %copy-start.3 = (f32[128,256]{1,0:T(8,128)S(1)}, f32[128,256]{1,0:T(8,128)}, u32[]{:S(2)}) copy-start(f32[128,256]{1,0:T(8,128)} %get-tuple-element.10) | copy-start | bytes 393220
Sparse Core Ops, SparseCore 0:
  44.9 352.3 all-reduce.5
  399.8 39.9 all-reduce.3
  442.7 46.4 reduce-scatter.1
